TPU v7x, 256 devices: a whole 4x4x8 slice. The times are simulated.
256 devices in a mesh: rows: 16 (over y_hi, x, core), feat: 16 (over y_lo, z).
Axes of the slice: x: 4, y: 4 (y_hi: 2, y_lo: 2; y = y_hi * 2 + y_lo), z: 8, core: 2. Of those that a mesh axis runs over, the one named last changes fastest.
Arguments:
- features: bfloat16 [3072, 16384], P('rows', 'feat'), may hold values from -0.5 to 0.5
- labels: int32 [3072], P('rows'), may hold values 0 or 1
- posterior: bfloat16 [16384], P('feat'), may hold values from -1 to 1
- prior_prec: float32 [16384], P('feat'), may hold values from 1 to 10
Outputs:
- hessian: float32 [16384, 16384], P('feat', 'rows')
- gradient: float32 [16384], P('feat')
All inputs are finite; a program needn't handle non-finite values. No bound on the sum of `labels` on one device may be relied on, other than what follows from the above.
Results may differ from a plain program's by a relative error of at most 0.003.
Values may be sent and summed in bfloat16 or wider, within the bound.
No kernel may reach another device: no remote copies, remote signals or barrier semaphores. Data moves between devices by JAX's collectives and lax.ppermute only.
A program may use at most 64 MiB of HBM per device.

v0:
```python
import jax
import jax.numpy as jnp
from jax import lax
from jax.sharding import PartitionSpec as P


def sent_to_all(x, axis):
    copies = jnp.broadcast_to(x, (lax.axis_size(axis), *x.shape))
    return lax.all_to_all(copies, axis, split_axis=0, concat_axis=0, tiled=True)


def over_copies(x, axis):
    return sent_to_all(x, axis).sum(axis=0)


def side_by_side(arrays, axis, dim, along):
    columns = [a.reshape(*a.shape[:along], -1) for a in arrays]
    both = jnp.concatenate(columns, axis=along)
    whole, at, finished = (lax.all_gather(both, axis, axis=dim, tiled=True), 0, [])
    for a, column in zip(arrays, columns):
        slab = whole[..., at : at + column.shape[along]]
        finished.append(slab.reshape(*slab.shape[:along], *a.shape[along:]))
        at += column.shape[along]
    return tuple(finished)


def per_device(features, labels, posterior, prior_prec):
    row_count = lax.axis_size("rows")
    feat_count = lax.axis_size("feat")
    row_index = lax.axis_index("rows")
    feat_index = lax.axis_index("feat")
    block_width = features.shape[1]
    col_width = block_width * feat_count // row_count
    partial_value = jnp.dot(features, posterior, preferred_element_type=jnp.float32)
    margins = over_copies(partial_value, "feat")
    chance = jax.nn.sigmoid(margins)
    weight = (chance * (1.0 - chance)).astype(jnp.bfloat16)
    residual = (labels.astype(jnp.float32) - chance).astype(jnp.bfloat16)
    all_rows, all_weight = side_by_side((features, weight), "rows", 0, 1)
    local_grad = jnp.dot(residual, features, preferred_element_type=jnp.float32)
    summed = over_copies(local_grad, "rows")
    gradient = summed - prior_prec * posterior.astype(jnp.float32)
    full_width = lax.all_gather(features, "feat", axis=1, tiled=True)
    column_rows = lax.all_to_all(full_width, "rows", split_axis=1, concat_axis=0, tiled=True)
    weighted = all_weight[:, None] * all_rows
    product = lax.dot_general(
        weighted, column_rows, (((0,), (0,)), ((), ())), preferred_element_type=jnp.float32
    )
    global_rows = feat_index * block_width + jnp.arange(block_width, dtype=jnp.int32)
    global_cols = row_index * col_width + jnp.arange(col_width, dtype=jnp.int32)
    on_diagonal = global_rows[:, None] == global_cols[None, :]
    hessian = product + jnp.where(on_diagonal, prior_prec[:, None], jnp.float32(0.0))
    return (hessian, gradient)


def solution(mesh):
    in_specs = (P("rows", "feat"), P("rows"), P("feat"), P("feat"))
    out_specs = (P("feat", "rows"), P("feat"))
    return jax.shard_map(
        per_device, mesh=mesh, in_specs=in_specs, out_specs=out_specs, check_vma=False
    )
```

profile of v0, /device:TPU:1, one launch (start us, length us, event | category | flops | bytes accessed | tf_op | source)
XLA Modules:
  0.0 242.4 jit_solution(10547593554285213768)
XLA Ops:
  7.2 0.0 all-gather.5.cloned.1.call-start
  7.2 0.7 all-gather.5.cloned.1.call-update
  7.9 0.0 all-gather.3.cloned.1.call-start
  7.9 0.7 reshape.56
  8.6 1.2 fusion.3
  9.9 17.3 %all_to_all.31 = f32[16,1,192]{2,1,0:T(1,128)S(1)} all-to-all(f32[16,1,192]{2,1,0:T(1,128)S(1)} %broadcast_in_dim.21), channel_id=1, replica_groups=mesh['rows'=16,'feat'=16] {'feat'}, dimensions={0} | all-to-all | bytes 24576 | tf_op jit(solution)/shard_map/all_to_all | solution.py:9
  27.2 0.7 subtract_convert_fusion
  27.9 0.2 copy.14
  28.0 1.8 pad_maximum_fusion
  29.8 0.0 all-gather.3.cloned.1.call-update
  29.9 1.2 fusion.4
  31.0 0.7 broadcast_in_dim.24
  31.7 8.8 %all-to-all-start.2 = ((f32[16,1,1024]{2,1,0:T(1,128)}), f32[16,1,1024]{2,1,0:T(1,128)S(1)}, u32[]{:S(2)}, u32[]{:S(2)}) async-start(f32[16,1,1024]{2,1,0:T(1,128)} %broadcast_in_dim.24), calls=%async_computation.2 | async-start | bytes 131072 | tf_op jit(solution)/shard_map/all_to_all | solution.py:9
  40.4 51.4 %all-gather.5.cloned.1.call-done = bf16[192,16384]{1,0:T(8,128)(2,1)} async-done(((bf16[192,1024]{1,0:T(8,128)(2,1)}), bf16[192,16384]{1,0:T(8,128)(2,1)}) %all-gather.5.cloned.1.call-update) | async-done | bytes 6291472 | tf_op jit(solution)/shard_map/all_gather | solution.py:43
  91.9 6.4 %copy.21 = bf16[24,16,8,1024]{3,2,0,1:T(8,128)(2,1)} copy(bf16[24,16,8,1024]{3,2,1,0:T(8,128)(2,1)} %bitcast.16) | data formatting | bytes 12582912 | tf_op jit(solution)/shard_map/all_to_all | solution.py:44
  98.3 0.0 all-to-all-done.2
  98.3 0.0 copy-start
  98.3 0.0 copy-start.1
  98.3 12.1 %all-to-all-start.1 = ((bf16[192,16,1024]{2,0,1:T(8,128)(2,1)}), bf16[192,16,1024]{2,0,1:T(8,128)(2,1)}, u32[]{:S(2)}, u32[]{:S(2)}) async-start(bf16[192,16,1024]{2,0,1:T(8,128)(2,1)} %bitcast.15), calls=%async_computation.1 | async-start | bytes 12582912 | tf_op jit(solution)/shard_map/all_to_all | solution.py:44
  110.4 0.1 reduce_sum.19
  110.5 0.0 copy-done
  110.5 0.0 copy-done.1
  110.5 0.6 multiply_subtract_fusion
  111.1 110.6 %all-gather.3.cloned.1.call-done = bf16[3072,1025]{1,0:T(8,128)(2,1)} async-done(((bf16[192,1025]{1,0:T(8,128)(2,1)}), bf16[3072,1025]{1,0:T(8,128)(2,1)}) %all-gather.3.cloned.1.call-update) | async-done | bytes 6297616 | tf_op jit(solution)/shard_map/all_gather | solution.py:19
  221.7 1.4 slice_reduce_fusion
  223.1 0.0 all-to-all-done.1
  223.1 12.5 %select_add_fusion = f32[1024,1024]{1,0:T(8,128)} fusion(bf16[3072,1024]{1,0:T(8,128)(2,1)} %bitcast.3, bf16[3072,1025]{1,0:T(8,128)(2,1)} %all-gather.3.cloned.1.call-done, bf16[3072]{0:T(1024)(128)(2,1)S(1)} %slice_reduce_fusion, f32[1024]{0:T(1024)S(1)} %copy-done.1, s32[1024]{0:T(1024)S(1)} %get-tuple-element.4, s32[1024]{0:T(1024)S(1)} %get-tuple-element.5), kind=kOutput, calls=%fused_computation.3 | convolution fusion | flops 6448742400 | bytes 16795648 | tf_op jit(solution)/shard_map/dot_general | solution.py:46
  (5 shorter events, 0.1 us)
Async XLA Ops:
  7.2 84.7 %all-gather.5.cloned.1.call-start = ((), (), s32[]{:S(2)}) async-start(), calls=%async_computation.4 | async-start | bytes 6684672 | tf_op jit(solution)/shard_map/all_gather | solution.py:43
  7.9 213.8 %all-gather.3.cloned.1.call-start = ((), (), s32[]{:S(2)}) async-start(), calls=%async_computation.3 | async-start | bytes 7520256 | tf_op jit(solution)/shard_map/all_gather | solution.py:19
  31.7 66.6 %all-to-all-start.2 = ((f32[16,1,1024]{2,1,0:T(1,128)}), f32[16,1,1024]{2,1,0:T(1,128)S(1)}, u32[]{:S(2)}, u32[]{:S(2)}) async-start(f32[16,1,1024]{2,1,0:T(1,128)} %broadcast_in_dim.24), calls=%async_computation.2 | async-start | bytes 131072 | tf_op jit(solution)/shard_map/all_to_all | solution.py:9
  98.3 12.2 %copy-start = (bf16[1024]{0:T(1024)(128)(2,1)S(1)}, bf16[1024]{0:T(1024)(128)(2,1)}, u32[]{:S(2)}) copy-start(bf16[1024]{0:T(1024)(128)(2,1)} %param.6) | copy-start | bytes 6148
  98.3 12.2 %copy-start.1 = (f32[1024]{0:T(1024)S(1)}, f32[1024]{0:T(1024)}, u32[]{:S(2)}) copy-start(f32[1024]{0:T(1024)} %param.7) | copy-start | bytes 12292
  98.3 124.8 %all-to-all-start.1 = ((bf16[192,16,1024]{2,0,1:T(8,128)(2,1)}), bf16[192,16,1024]{2,0,1:T(8,128)(2,1)}, u32[]{:S(2)}, u32[]{:S(2)}) async-start(bf16[192,16,1024]{2,0,1:T(8,128)(2,1)} %bitcast.15), calls=%async_computation.1 | async-start | bytes 12582912 | tf_op jit(solution)/shard_map/all_to_all | solution.py:44
Sparse Core Ops, SparseCore 0:
  9.8 82.0 all-gather.4
  95.2 126.4 all-gather.2
where the time goes:
time: 243 us; the launch traced here: 242 us
  waiting for transfers between devices  163 us (67%)
  starting transfers between devices  21 us (9%)
  blocking collectives  17.3 us (7%)
  matrix products  14.8 us (6%)
  between operations  14.1 us (6%)
  local copies, waits for them, and re-layouts  9.38 us (4%)
  other arithmetic  3.19 us (1%)
    all_gather x1, waiting for transfers between devices, side_by_side(): lax.all_gather(both, axis, axis=dim, tiled=True)  111 us
    all_gather x1, waiting for transfers between devices, per_device(): full_width = lax.all_gather(features, 'feat', axis=1, tiled=True)  51.4 us
    all_to_all x1, blocking collectives, sent_to_all(): return lax.all_to_all(copies, axis, split_axis=0, concat_axis=0, tiled=True)  17.3 us
    dot_general x1, matrix products, per_device(): lax.dot_general(weighted, column_rows, (((0,), (0,)), ((), ())), preferre...  12.5 us
    all_to_all x1, starting transfers between devices, per_device(): lax.all_to_all(full_width, 'rows', split_axis=1, concat_axis=0, tiled=True)  12.1 us
    all_to_all x1, starting transfers between devices, sent_to_all(): return lax.all_to_all(copies, axis, split_axis=0, concat_axis=0, tiled=True)  8.76 us
    all_to_all x1, local copies, waits for them, and re-layouts, per_device(): lax.all_to_all(full_width, 'rows', split_axis=1, concat_axis=0, tiled=True)  6.42 us
  transfers between devices with their start and end apart: 4, of which 2 were waited for; matrix products, arithmetic and copies ran while one was open for 6% of the time, Pallas kernels for 0%

commit v1 on v0

--- a/solution.py
+++ b/solution.py
@@ -40,7 +40,9 @@
     local_grad = jnp.dot(residual, features, preferred_element_type=jnp.float32)
     summed = over_copies(local_grad, "rows")
     gradient = summed - prior_prec * posterior.astype(jnp.float32)
-    full_width = lax.all_gather(features, "feat", axis=1, tiled=True)
+    full_width = jnp.concatenate(
+        lax.all_to_all(jnp.stack([features] * lax.axis_size("feat")), "feat", 0, 0), axis=1
+    )
     column_rows = lax.all_to_all(full_width, "rows", split_axis=1, concat_axis=0, tiled=True)
     weighted = all_weight[:, None] * all_rows
     product = lax.dot_general(

time: 243 us -> 305 us (1.26)
  waiting for transfers between devices: 163 us -> 221 us
  blocking collectives: 17.3 us -> 33.1 us
  starting transfers between devices: 21 us -> 10.4 us
    all_to_all x1, waiting for transfers between devices: 0.01 us -> 139 us  [per_device(): lax.all_to_all(jnp.stack([features] * lax.axis_size('feat')), 'feat', 0, 0)]
    all_gather x1, waiting for transfers between devices: 111 us -> 0.01 us  [side_by_side(): lax.all_gather(both, axis, axis=dim, tiled=True)]
    all_to_all x1, waiting for transfers between devices: 0.01 us -> 82.1 us  [per_device(): lax.all_to_all(full_width, 'rows', split_axis=1, concat_axis=0, tiled=True)]
    all_gather x1 -> x0, waiting for transfers between devices: 51.4 us -> none  [per_device(): full_width = lax.all_gather(features, 'feat', axis=1, tiled=True)]
    all_to_all x1 -> x2, blocking collectives: 17.3 us -> 33.1 us  [sent_to_all(): return lax.all_to_all(copies, axis, split_axis=0, concat_axis=0, tiled=True)]
    all_to_all x1, starting transfers between devices: 12.1 us -> 5.58 us  [per_device(): lax.all_to_all(full_width, 'rows', split_axis=1, concat_axis=0, tiled=True)]
    all_to_all x1 -> x0, local copies, waits for them, and re-layouts: 6.42 us -> none  [per_device(): lax.all_to_all(full_width, 'rows', split_axis=1, concat_axis=0, tiled=True)]
    another operation x0 -> x1, local copies, waits for them, and re-layouts: none -> 4.39 us  [per_device(): jnp.stack([features] * lax.axis_size('feat'))]
  transfers between devices with their start and end apart: 4 -> 3, of which waited for: 2 -> 2; matrix products, arithmetic and copies ran while one was open for 6% -> 1% of each run, Pallas kernels for 0% -> 0%
where the time goes in v1:
time: 305 us; the launch traced here: 302 us
  waiting for transfers between devices  221 us (72%)
  blocking collectives  33.1 us (11%)
  matrix products  14.8 us (5%)
  between operations  14.1 us (5%)
  starting transfers between devices  10.4 us (3%)
  local copies, waits for them, and re-layouts  6.73 us (2%)
    all_to_all x1, waiting for transfers between devices, per_device(): lax.all_to_all(jnp.stack([features] * lax.axis_size('feat')), 'feat', 0, 0)  139 us
    all_to_all x1, waiting for transfers between devices, per_device(): lax.all_to_all(full_width, 'rows', split_axis=1, concat_axis=0, tiled=True)  82.1 us
    all_to_all x2, blocking collectives, sent_to_all(): return lax.all_to_all(copies, axis, split_axis=0, concat_axis=0, tiled=True)  33.1 us
    dot_general x1, matrix products, per_device(): lax.dot_general(weighted, column_rows, (((0,), (0,)), ((), ())), preferre...  12.4 us
  transfers between devices with their start and end apart: 3, of which 2 were waited for; matrix products, arithmetic and copies ran while one was open for 1% of the time, Pallas kernels for 0%

profile of v1, /device:TPU:1, one launch (start us, length us, event | category | flops | bytes accessed | tf_op | source)
XLA Modules:
  0.0 302.5 jit_solution(15596093347263968525)
XLA Ops:
  7.2 0.7 reshape.64
  7.9 1.2 fusion.3
  9.1 17.3 %all_to_all.33 = f32[16,1,192]{2,1,0:T(1,128)S(1)} all-to-all(f32[16,1,192]{2,1,0:T(1,128)S(1)} %broadcast_in_dim.21), channel_id=1, replica_groups=mesh['rows'=16,'feat'=16] {'feat'}, dimensions={0} | all-to-all | bytes 24576 | tf_op jit(solution)/shard_map/all_to_all | solution.py:9
  26.4 0.7 subtract_convert_fusion
  27.1 1.2 fusion.4
  28.3 15.9 %all_to_all.34 = f32[16,1,1024]{2,1,0:T(1,128)S(1)} all-to-all(f32[16,1,1024]{2,1,0:T(1,128)S(1)} %broadcast_in_dim.24), channel_id=1, replica_groups=mesh['rows'=16,'feat'=16] {'rows'}, dimensions={0} | all-to-all | bytes 131072 | tf_op jit(solution)/shard_map/all_to_all | solution.py:9
  44.2 4.4 %stack.2 = bf16[16,192,1024]{2,1,0:T(8,128)(2,1)} broadcast(bf16[192,1024]{1,0:T(8,128)(2,1)} %param.4), dimensions={1,2} | broadcast | bytes 6684672 | tf_op jit(solution)/shard_map/stack | solution.py:44
  48.6 0.0 copy-start
  48.6 4.8 %all-to-all-start.1 = ((bf16[16,192,1024]{2,1,0:T(8,128)(2,1)}), bf16[16,192,1024]{2,1,0:T(8,128)(2,1)}, u32[]{:S(2)}, u32[]{:S(2)}) async-start(bf16[16,192,1024]{2,1,0:T(8,128)(2,1)} %stack.2), calls=%async_computation.1 | async-start | bytes 12582912 | tf_op jit(solution)/shard_map/all_to_all | solution.py:44
  53.3 0.0 all-gather.2.cloned.1.call-start
  53.4 0.1 copy.9
  53.6 0.0 copy-done
  53.6 0.8 pad_maximum_fusion
  54.4 0.0 all-gather.2.cloned.1.call-update
  54.4 139.0 %all-to-all-done.1 = bf16[16,192,1024]{2,1,0:T(8,128)(2,1)} async-done(((bf16[16,192,1024]{2,1,0:T(8,128)(2,1)}), bf16[16,192,1024]{2,1,0:T(8,128)(2,1)}, u32[]{:S(2)}, u32[]{:S(2)}) %all-to-all-start.1) | async-done | bytes 6291488 | tf_op jit(solution)/shard_map/all_to_all | solution.py:44
  193.3 0.0 copy-start.1
  193.3 0.0 copy-start.2
  193.3 5.6 %all-to-all-start.2 = ((bf16[192,16,1024]{2,0,1:T(8,128)(2,1)}), bf16[192,16,1024]{2,0,1:T(8,128)(2,1)}, u32[]{:S(2)}, u32[]{:S(2)}) async-start(bf16[192,16,1024]{2,0,1:T(8,128)(2,1)} %bitcast.2), calls=%async_computation.2 | async-start | bytes 12582912 | tf_op jit(solution)/shard_map/all_to_all | solution.py:46
  198.9 0.1 reduce_sum.19
  199.0 0.0 copy-done.1
  199.0 0.0 copy-done.2
  199.0 0.6 multiply_subtract_fusion
  199.6 0.0 all-gather.2.cloned.1.call-done
  199.6 1.4 slice_reduce_fusion
  201.0 82.1 %all-to-all-done.2 = bf16[192,16,1024]{2,0,1:T(8,128)(2,1)} async-done(((bf16[192,16,1024]{2,0,1:T(8,128)(2,1)}), bf16[192,16,1024]{2,0,1:T(8,128)(2,1)}, u32[]{:S(2)}, u32[]{:S(2)}) %all-to-all-start.2) | async-done | bytes 6291488 | tf_op jit(solution)/shard_map/all_to_all | solution.py:46
  283.2 12.4 %select_add_fusion = f32[1024,1024]{1,0:T(8,128)} fusion(bf16[3072,1024]{1,0:T(8,128)(2,1)} %bitcast.4, bf16[3072,1025]{1,0:T(8,128)(2,1)} %all-gather.2.cloned.1.call-done, bf16[3072]{0:T(1024)(128)(2,1)S(1)} %slice_reduce_fusion, f32[1024]{0:T(1024)S(1)} %copy-done.2, s32[1024]{0:T(1024)S(1)} %get-tuple-element.4, s32[1024]{0:T(1024)S(1)} %get-tuple-element.5), kind=kOutput, calls=%fused_computation.2 | convolution fusion | flops 6448742400 | bytes 16795648 | tf_op jit(solution)/shard_map/dot_general | solution.py:48
  (6 shorter events, 0.1 us)
Async XLA Ops:
  48.6 5.0 %copy-start = (bf16[192,1024]{1,0:T(8,128)(2,1)S(1)}, bf16[192,1024]{1,0:T(8,128)(2,1)}, u32[]{:S(2)}) copy-start(bf16[192,1024]{1,0:T(8,128)(2,1)} %param.4) | copy-start | bytes 1179652
  48.6 144.8 %all-to-all-start.1 = ((bf16[16,192,1024]{2,1,0:T(8,128)(2,1)}), bf16[16,192,1024]{2,1,0:T(8,128)(2,1)}, u32[]{:S(2)}, u32[]{:S(2)}) async-start(bf16[16,192,1024]{2,1,0:T(8,128)(2,1)} %stack.2), calls=%async_computation.1 | async-start | bytes 12582912 | tf_op jit(solution)/shard_map/all_to_all | solution.py:44
  53.3 146.3 %all-gather.2.cloned.1.call-start = ((), (), s32[]{:S(2)}) async-start(), calls=%async_computation.4 | async-start | bytes 7520256 | tf_op jit(solution)/shard_map/all_gather | solution.py:19
  193.3 5.7 %copy-start.1 = (bf16[1024]{0:T(1024)(128)(2,1)S(1)}, bf16[1024]{0:T(1024)(128)(2,1)}, u32[]{:S(2)}) copy-start(bf16[1024]{0:T(1024)(128)(2,1)} %param.6) | copy-start | bytes 6148
  193.3 5.7 %copy-start.2 = (f32[1024]{0:T(1024)S(1)}, f32[1024]{0:T(1024)}, u32[]{:S(2)}) copy-start(f32[1024]{0:T(1024)} %param.7) | copy-start | bytes 12292
  193.3 89.8 %all-to-all-start.2 = ((bf16[192,16,1024]{2,0,1:T(8,128)(2,1)}), bf16[192,16,1024]{2,0,1:T(8,128)(2,1)}, u32[]{:S(2)}, u32[]{:S(2)}) async-start(bf16[192,16,1024]{2,0,1:T(8,128)(2,1)} %bitcast.2), calls=%async_computation.2 | async-start | bytes 12582912 | tf_op jit(solution)/shard_map/all_to_all | solution.py:46
Sparse Core Ops, SparseCore 0:
  57.5 113.5 all-gather.1

commit v2 on v0

--- a/solution.py
+++ b/solution.py
@@ -41,7 +41,12 @@
     summed = over_copies(local_grad, "rows")
     gradient = summed - prior_prec * posterior.astype(jnp.float32)
     full_width = lax.all_gather(features, "feat", axis=1, tiled=True)
-    column_rows = lax.all_to_all(full_width, "rows", split_axis=1, concat_axis=0, tiled=True)
+    column_rows = jnp.concatenate(
+        lax.all_to_all(
+            jnp.stack(jnp.split(full_width, lax.axis_size("rows"), axis=1)), "rows", 0, 0
+        ),
+        axis=0,
+    )
     weighted = all_weight[:, None] * all_rows
     product = lax.dot_general(
         weighted, column_rows, (((0,), (0,)), ((), ())), preferred_element_type=jnp.float32

time: 243 us -> 257 us (1.058)
  local copies, waits for them, and re-layouts: 9.38 us -> 31.4 us
  waiting for transfers between devices: 163 us -> 154 us
    unnamed x5 -> x20, local copies, waits for them, and re-layouts: 0.7 us -> 27.3 us
    all_gather x1, waiting for transfers between devices: 111 us -> 102 us  [side_by_side(): lax.all_gather(both, axis, axis=dim, tiled=True)]
    all_to_all x1 -> x0, local copies, waits for them, and re-layouts: 6.42 us -> none  [per_device(): lax.all_to_all(full_width, 'rows', split_axis=1, concat_axis=0, tiled=True)]
  transfers between devices with their start and end apart: 4 -> 4, of which waited for: 2 -> 2; matrix products, arithmetic and copies ran while one was open for 6% -> 14% of each run, Pallas kernels for 0% -> 0%
where the time goes in v2:
time: 257 us; the launch traced here: 256 us
  waiting for transfers between devices  154 us (60%)
  local copies, waits for them, and re-layouts  31.4 us (12%)
  starting transfers between devices  21 us (8%)
  blocking collectives  17.3 us (7%)
  matrix products  14.8 us (6%)
  between operations  14.1 us (5%)
  other arithmetic  3.19 us (1%)
    all_gather x1, waiting for transfers between devices, side_by_side(): lax.all_gather(both, axis, axis=dim, tiled=True)  102 us
    all_gather x1, waiting for transfers between devices, per_device(): full_width = lax.all_gather(features, 'feat', axis=1, tiled=True)  51.4 us
    unnamed x20, local copies, waits for them, and re-layouts  27.3 us
    all_to_all x1, blocking collectives, sent_to_all(): return lax.all_to_all(copies, axis, split_axis=0, concat_axis=0, tiled=True)  17.3 us
    dot_general x1, matrix products, per_device(): lax.dot_general(weighted, column_rows, (((0,), (0,)), ((), ())), preferre...  12.5 us
    all_to_all x1, starting transfers between devices, per_device(): lax.all_to_all(jnp.stack(jnp.split(full_width, lax.axis_size('rows'), axi...  12.2 us
    all_to_all x1, starting transfers between devices, sent_to_all(): return lax.all_to_all(copies, axis, split_axis=0, concat_axis=0, tiled=True)  8.76 us
  transfers between devices with their start and end apart: 4, of which 2 were waited for; matrix products, arithmetic and copies ran while one was open for 14% of the time, Pallas kernels for 0%

profile of v2, /device:TPU:1, one launch (start us, length us, event | category | flops | bytes accessed | tf_op | source)
XLA Modules:
  0.0 255.6 jit_solution(4107302911086472247)
XLA Ops:
  7.2 0.7 all-gather.5.cloned.1.call-update
  7.9 0.7 reshape.57
  8.6 1.2 fusion.19
  9.9 17.3 %all_to_all.17 = f32[16,1,192]{2,1,0:T(1,128)S(1)} all-to-all(f32[16,1,192]{2,1,0:T(1,128)S(1)} %broadcast_in_dim.21), channel_id=1, replica_groups=mesh['rows'=16,'feat'=16] {'feat'}, dimensions={0} | all-to-all | bytes 24576 | tf_op jit(solution)/shard_map/all_to_all | solution.py:9
  27.2 0.7 subtract_convert_fusion
  27.9 0.2 copy.9
  28.0 1.8 pad_maximum_fusion
  29.9 1.2 fusion.20
  31.0 0.7 broadcast_in_dim.24
  31.7 8.8 %all-to-all-start.2 = ((f32[16,1,1024]{2,1,0:T(1,128)}), f32[16,1,1024]{2,1,0:T(1,128)S(1)}, u32[]{:S(2)}, u32[]{:S(2)}) async-start(f32[16,1,1024]{2,1,0:T(1,128)} %broadcast_in_dim.24), calls=%async_computation.2 | async-start | bytes 131072 | tf_op jit(solution)/shard_map/all_to_all | solution.py:9
  40.4 51.4 %all-gather.5.cloned.1.call-done = bf16[192,16384]{1,0:T(8,128)(2,1)} async-done(((bf16[192,1024]{1,0:T(8,128)(2,1)}), bf16[192,16384]{1,0:T(8,128)(2,1)}) %all-gather.5.cloned.1.call-update) | async-done | bytes 6291472 | tf_op jit(solution)/shard_map/all_gather | solution.py:43
  91.9 1.8 fusion.17
  93.7 1.8 fusion.16
  95.4 1.8 fusion.15
  97.2 1.8 fusion.14
  99.0 1.8 fusion.13
  100.8 1.8 fusion.12
  102.5 1.8 fusion.11
  104.3 1.8 fusion.10
  106.1 1.8 fusion.9
  107.8 1.8 fusion.8
  109.6 1.8 fusion.7
  111.4 1.8 fusion.6
  113.2 1.8 fusion.5
  115.0 1.8 fusion.4
  116.7 1.8 fusion.3
  118.5 1.8 fusion.2
  120.3 12.2 %all-to-all-start.1 = ((bf16[16,192,1024]{2,1,0:T(8,128)(2,1)}), bf16[16,192,1024]{2,1,0:T(8,128)(2,1)}, u32[]{:S(2)}, u32[]{:S(2)}) async-start(bf16[16,192,1024]{2,1,0:T(8,128)(2,1)} %fusion.2), calls=%async_computation.1 | async-start | bytes 12582912 | tf_op jit(solution)/shard_map/all_to_all | solution.py:45
  132.6 0.6 multiply_subtract_fusion
  133.2 101.8 %all-gather.3.cloned.1.call-done = bf16[3072,1025]{1,0:T(8,128)(2,1)} async-done(((bf16[192,1025]{1,0:T(8,128)(2,1)}), bf16[3072,1025]{1,0:T(8,128)(2,1)}) %all-gather.3.cloned.1.call-update) | async-done | bytes 6297616 | tf_op jit(solution)/shard_map/all_gather | solution.py:19
  234.9 1.4 slice_reduce_fusion
  236.3 12.5 %select_add_fusion = f32[1024,1024]{1,0:T(8,128)} fusion(bf16[3072,1024]{1,0:T(8,128)(2,1)} %bitcast.18, bf16[3072,1025]{1,0:T(8,128)(2,1)} %all-gather.3.cloned.1.call-done, bf16[3072]{0:T(1024)(128)(2,1)S(1)} %slice_reduce_fusion, f32[1024]{0:T(1024)S(1)} %copy-done.1, s32[1024]{0:T(1024)S(1)} %get-tuple-element.4, s32[1024]{0:T(1024)S(1)} %get-tuple-element.5), kind=kOutput, calls=%fused_computation.2 | convolution fusion | flops 6448742400 | bytes 16795648 | tf_op jit(solution)/shard_map/dot_general | solution.py:51
  (15 shorter events, 0.2 us)
Async XLA Ops:
  7.2 84.7 %all-gather.5.cloned.1.call-start = ((), (), s32[]{:S(2)}) async-start(), calls=%async_computation.4 | async-start | bytes 6684672 | tf_op jit(solution)/shard_map/all_gather | solution.py:43
  7.9 227.0 %all-gather.3.cloned.1.call-start = ((), (), s32[]{:S(2)}) async-start(), calls=%async_computation.3 | async-start | bytes 7520256 | tf_op jit(solution)/shard_map/all_gather | solution.py:19
  31.7 88.6 %all-to-all-start.2 = ((f32[16,1,1024]{2,1,0:T(1,128)}), f32[16,1,1024]{2,1,0:T(1,128)S(1)}, u32[]{:S(2)}, u32[]{:S(2)}) async-start(f32[16,1,1024]{2,1,0:T(1,128)} %broadcast_in_dim.24), calls=%async_computation.2 | async-start | bytes 131072 | tf_op jit(solution)/shard_map/all_to_all | solution.py:9
  120.3 12.3 %copy-start = (bf16[1024]{0:T(1024)(128)(2,1)S(1)}, bf16[1024]{0:T(1024)(128)(2,1)}, u32[]{:S(2)}) copy-start(bf16[1024]{0:T(1024)(128)(2,1)} %param.6) | copy-start | bytes 6148
  120.3 12.3 %copy-start.1 = (f32[1024]{0:T(1024)S(1)}, f32[1024]{0:T(1024)}, u32[]{:S(2)}) copy-start(f32[1024]{0:T(1024)} %param.7) | copy-start | bytes 12292
  120.3 116.1 %all-to-all-start.1 = ((bf16[16,192,1024]{2,1,0:T(8,128)(2,1)}), bf16[16,192,1024]{2,1,0:T(8,128)(2,1)}, u32[]{:S(2)}, u32[]{:S(2)}) async-start(bf16[16,192,1024]{2,1,0:T(8,128)(2,1)} %fusion.2), calls=%async_computation.1 | async-start | bytes 12582912 | tf_op jit(solution)/shard_map/all_to_all | solution.py:45
Sparse Core Ops, SparseCore 0:
  9.8 82.0 all-gather.4
  95.2 139.7 all-gather.2
